TPU v7x, 128 devices: a whole 4x4x4 slice. The times are simulated.
128 devices in a mesh: gx: 8 (over z, x_lo), gy: 16 (over x_hi, y, core).
Axes of the slice: x: 4 (x_hi: 2, x_lo: 2; x = x_hi * 2 + x_lo), y: 4, z: 4, core: 2. Of those that a mesh axis runs over, the one named last changes fastest.
Arguments:
- fields: float32 [6, 256, 512, 128], P(None, 'gx', 'gy'), may hold values from -6 to 6
- eps_background: float32 [256, 512, 128], P('gx', 'gy'), may hold values from 1 to 4
- target: float32 [256, 256], replicated, may hold values from 1 to 10
- widths: float32 [16384], P(('gx', 'gy')), may hold values from 0.2 to 1
- intersection: float32 [16384, 16], P(('gx', 'gy')), may hold values from 0.1 to 1
- pillar_tile: int32 [16384, 1], P(('gx', 'gy')), may hold values from 0 to 127; in each aligned block of 128 rows (0 to 127, 128 to 255, ...) at most 2 rows name the same one
- anchors: int32 [16384, 2], P(('gx', 'gy')), may hold values from 0 to 28
Outputs:
- final_fields: float32 [6, 256, 512, 128], P(None, 'gx', 'gy')
- focal_power: float32 [256, 256], P(('gx', 'gy'))
- grad_widths: float32 [16384], P(('gx', 'gy'))
Inputs may be any that keep to these rules, and one draw needn't show every extreme that they name: `pillar_tile`: in the pillars of one device (aligned blocks of 128), no tile is named by more than 2 pillars, a bound that some block reaches. Tile t is the one at gx index t div (512 div 32) and gy index t mod (512 div 32).
All inputs are finite; a program needn't handle non-finite values.
Results may differ from a plain program's by a relative error of at most 0.00016.
Values sent between devices are 32-bit elements; how exact they have to be, the bound alone decides.
A program may use at most 128 MiB of HBM per device.

v0:
```python
import math

import jax
import jax.numpy as jnp
from jax import lax
from jax.sharding import PartitionSpec as P

TILE = 32
P_DEV = 128
NT = 4
ZP = 4
U = 256
V = 256
ZM = 64


COURANT = 0.5
ANGULAR_STEP = 0.9
DELTA_EPS = 4.0


def passed_along(shard, axis, by):
    count = lax.axis_size(axis)
    pairs = [(i, i + by) for i in range(count) if 0 <= i + by < count]
    return lax.ppermute(shard, axis, pairs)


def plus_diff(field, rim_layer, axis):
    extended = jnp.concatenate([field, rim_layer], axis=axis)
    return lax.slice_in_dim(extended, 1, extended.shape[axis], axis=axis) - field


def minus_diff(field, rim_layer, axis):
    extended = jnp.concatenate([rim_layer, field], axis=axis)
    return field - lax.slice_in_dim(extended, 0, field.shape[axis], axis=axis)


def leap_step(fields_now, inv_eps, sources):
    elec_x, elec_y, elec_z, magn_x, magn_y, magn_z = fields_now
    z_blank = jnp.zeros_like(elec_x[:, :, :1])
    rim_east = passed_along(jnp.stack([elec_y[:1], elec_z[:1]]), "gx", -1)
    rim_north = passed_along(jnp.stack([elec_x[:, :1], elec_z[:, :1]]), "gy", -1)
    curl_x = plus_diff(elec_z, rim_north[1], 1) - plus_diff(elec_y, z_blank, 2)
    curl_y = plus_diff(elec_x, z_blank, 2) - plus_diff(elec_z, rim_east[1], 0)
    curl_z = plus_diff(elec_y, rim_east[0], 0) - plus_diff(elec_x, rim_north[0], 1)
    magn_x = magn_x - COURANT * curl_x
    magn_y = magn_y - COURANT * curl_y
    magn_z = magn_z - COURANT * curl_z
    rim_west = passed_along(jnp.stack([magn_y[-1:], magn_z[-1:]]), "gx", 1)
    rim_south = passed_along(jnp.stack([magn_x[:, -1:], magn_z[:, -1:]]), "gy", 1)
    curl_x = minus_diff(magn_z, rim_south[1], 1) - minus_diff(magn_y, z_blank, 2)
    curl_y = minus_diff(magn_x, z_blank, 2) - minus_diff(magn_z, rim_west[1], 0)
    curl_z = minus_diff(magn_y, rim_west[0], 0) - minus_diff(magn_x, rim_south[0], 1)
    elec_x = elec_x + COURANT * (curl_x - sources[0]) * inv_eps
    elec_y = elec_y + COURANT * (curl_y - sources[1]) * inv_eps
    elec_z = elec_z + COURANT * curl_z * inv_eps
    return (elec_x, elec_y, elec_z, magn_x, magn_y, magn_z)


def kernel_table(count_out, count_in, offset, length):
    focal_pos = (jnp.arange(count_out, dtype=jnp.float32) + 0.5) / count_out - 0.5
    cell_pos = (
        offset.astype(jnp.float32) + jnp.arange(length, dtype=jnp.float32) + 0.5
    ) / count_in - 0.5
    phase = math.pi * count_out * (focal_pos[:, None] - cell_pos[None, :]) ** 2
    return (jnp.cos(phase), jnp.sin(phase))


def contract(pattern, first_op, second_op):
    return jnp.einsum(pattern, first_op, second_op, precision=lax.Precision.HIGHEST)


def project_forward(mon_re, mon_im, table_x, table_y, norm_scale):
    x_re, x_im = table_x
    y_re, y_im = table_y
    part_re = contract("ux,cxy->cuy", x_re, mon_re) - contract("ux,cxy->cuy", x_im, mon_im)
    part_im = contract("ux,cxy->cuy", x_re, mon_im) + contract("ux,cxy->cuy", x_im, mon_re)
    far_re = contract("cuy,vy->cuv", part_re, y_re) - contract("cuy,vy->cuv", part_im, y_im)
    far_im = contract("cuy,vy->cuv", part_re, y_im) + contract("cuy,vy->cuv", part_im, y_re)
    return norm_scale * jnp.stack([far_re, far_im])


def project_back(weighted, table_x, table_y, norm_scale):
    x_re, x_im = table_x
    y_re, y_im = table_y
    w_re = weighted[0]
    w_im = weighted[1]
    half_re = contract("cuv,vy->cuy", w_re, y_re) - contract("cuv,vy->cuy", w_im, y_im)
    half_im = contract("cuv,vy->cuy", w_re, y_im) + contract("cuv,vy->cuy", w_im, y_re)
    back_re = contract("ux,cuy->cxy", x_re, half_re) - contract("ux,cuy->cxy", x_im, half_im)
    back_im = contract("ux,cuy->cxy", x_re, half_im) + contract("ux,cuy->cxy", x_im, half_re)
    return (2.0 * norm_scale * back_re, 2.0 * norm_scale * back_im)


def shards(fields, eps_background, target, widths, intersection, pillar_tile, anchors):
    span_x = lax.axis_size("gx")
    span_y = lax.axis_size("gy")
    devices = span_x * span_y
    place_x = lax.axis_index("gx")
    place_y = lax.axis_index("gy")
    linear = place_x * span_y + place_y
    offsets = jnp.arange(16, dtype=jnp.int32)
    capacity = 2 * max(1, P_DEV // devices)
    target_tile = pillar_tile[:, 0]
    onehot = (target_tile[:, None] == jnp.arange(devices, dtype=jnp.int32)[None, :]).astype(
        jnp.int32
    )
    earlier = jnp.cumsum(onehot, axis=0) - onehot
    order_in = jnp.sum(earlier * onehot, axis=1)
    slot_ids = target_tile * capacity + order_in
    packed = (
        jnp.zeros((devices * capacity, 16), jnp.float32)
        .at[slot_ids]
        .set(intersection * widths[:, None])
    )
    packed_at = (
        jnp.zeros((devices * capacity, 2), jnp.float32)
        .at[slot_ids]
        .set(anchors.astype(jnp.float32))
    )
    got_vals, got_at = (
        lax.all_to_all(
            packed.reshape(devices, capacity, 16),
            ("gx", "gy"),
            split_axis=0,
            concat_axis=0,
            tiled=True,
        ),
        lax.all_to_all(
            packed_at.reshape(devices, capacity, 2),
            ("gx", "gy"),
            split_axis=0,
            concat_axis=0,
            tiled=True,
        ),
    )
    local_vals = got_vals.reshape(devices * capacity, 16)
    local_at = got_at.reshape(devices * capacity, 2).astype(jnp.int32)
    cells_x = local_at[:, 0:1] + (offsets // 4)[None, :]
    cells_y = local_at[:, 1:2] + (offsets % 4)[None, :]
    filling = jnp.zeros((TILE, TILE), jnp.float32).at[cells_x, cells_y].add(local_vals)
    z_index = jnp.arange(fields.shape[3], dtype=jnp.int32)
    layers = ((z_index >= ZM - ZP) & (z_index < ZM)).astype(jnp.float32)
    permittivity = eps_background + DELTA_EPS * filling[:, :, None] * layers[None, None, :]
    inv_eps = 1.0 / permittivity
    blank = jnp.zeros_like(eps_background)
    fields_now = tuple((fields[component] for component in range(6)))
    mon_re = jnp.zeros((2, TILE, TILE), jnp.float32)
    mon_im = jnp.zeros((2, TILE, TILE), jnp.float32)
    changes = []
    for moment in range(1, NT + 1):
        before = fields_now[:3]
        fields_now = leap_step(fields_now, inv_eps, (blank, blank, blank))
        monitor = jnp.stack([fields_now[0][:, :, ZM], fields_now[1][:, :, ZM]])
        mon_re = mon_re + math.cos(ANGULAR_STEP * moment) * monitor
        mon_im = mon_im - math.sin(ANGULAR_STEP * moment) * monitor
        changes.append(
            tuple(
                (
                    (fields_now[component] - before[component])[:, :, ZM - ZP : ZM]
                    for component in range(3)
                )
            )
        )
    norm_scale = (TILE * span_x * TILE * span_y) ** (-0.5)
    table_x = kernel_table(U, TILE * span_x, place_x * TILE, TILE)
    table_y = kernel_table(V, TILE * span_y, place_y * TILE, TILE)
    row_count = U // devices
    row_start = linear * row_count
    partial_far = project_forward(mon_re, mon_im, table_x, table_y, norm_scale)
    far_field = lax.psum(partial_far, ("gx", "gy"))
    mine_rows = lax.dynamic_slice_in_dim(far_field, row_start, row_count, 2)
    focal_power = jnp.sum(mine_rows * mine_rows, axis=(0, 1))
    weighted = jnp.stack([target * far_field[0], -(target * far_field[1])])
    back_re, back_im = project_back(weighted, table_x, table_y, norm_scale)
    adjoint = tuple((blank for component in range(6)))
    inv_layer = inv_eps[:, :, ZM - ZP : ZM]
    grad_eps = jnp.zeros((TILE, TILE, ZP), jnp.float32)
    for moment in range(1, NT + 1):
        source_step = NT + 1 - moment
        adj_drive = (
            math.cos(ANGULAR_STEP * source_step) * back_re
            + math.sin(ANGULAR_STEP * source_step) * back_im
        )
        source_x = blank.at[:, :, ZM].set(adj_drive[0])
        source_y = blank.at[:, :, ZM].set(adj_drive[1])
        adjoint = leap_step(adjoint, inv_eps, (source_x, source_y, blank))
        change = changes[source_step - 1]
        product = (
            adjoint[0][:, :, ZM - ZP : ZM] * change[0]
            + adjoint[1][:, :, ZM - ZP : ZM] * change[1]
            + adjoint[2][:, :, ZM - ZP : ZM] * change[2]
        )
        grad_eps = grad_eps - product * inv_layer
    column_grad = jnp.sum(grad_eps, axis=2)
    picked = column_grad[cells_x, cells_y]
    returned = lax.all_to_all(
        picked.reshape(devices, capacity, 16), ("gx", "gy"), split_axis=0, concat_axis=0, tiled=True
    )
    own_vals = returned.reshape(devices * capacity, 16)[slot_ids]
    grad_widths = DELTA_EPS * jnp.sum(intersection * own_vals, axis=1)
    return (jnp.stack(fields_now), focal_power, grad_widths)


def solution(mesh):
    placed = (
        P(None, "gx", "gy", None),
        P("gx", "gy", None),
        P(),
        P(("gx", "gy")),
        P(("gx", "gy"), None),
        P(("gx", "gy"), None),
        P(("gx", "gy"), None),
    )
    return jax.shard_map(
        shards,
        mesh=mesh,
        in_specs=placed,
        out_specs=(P(None, "gx", "gy", None), P(("gx", "gy"), None), P(("gx", "gy"))),
        check_vma=False,
    )
```

profile of v0, /device:TPU:1, one launch (start us, length us, event | category | flops | bytes accessed | tf_op | source)
XLA Modules:
  0.0 479.0 jit_solution(2018501460073034488)
XLA Ops:
  9.4 3.3 collective-permute-start.17
  18.3 12.4 %all-to-all-start = ((f32[128,2,2]{1,2,0:T(2,128)}), f32[128,2,2]{1,2,0:T(2,128)S(1)}, u32[]{:S(2)}, u32[]{:S(2)}) async-start(f32[128,2,2]{1,2,0:T(2,128)} %copy.4958), calls=%async_computation | async-start | bytes 262144 | tf_op jit(solution)/shard_map/all_to_all | solution.py:129
  42.3 11.5 %all-to-all-start.1 = ((f32[128,2,16]{2,1,0:T(2,128)}), f32[128,2,16]{2,1,0:T(2,128)S(1)}, u32[]{:S(2)}, u32[]{:S(2)}) async-start(f32[128,2,16]{2,1,0:T(2,128)} %bitcast.24), calls=%async_computation.1 | async-start | bytes 262144 | tf_op jit(solution)/shard_map/all_to_all | solution.py:122
  56.7 7.2 %all-to-all-done.1 = f32[128,2,16]{2,1,0:T(2,128)S(1)} async-done(((f32[128,2,16]{2,1,0:T(2,128)}), f32[128,2,16]{2,1,0:T(2,128)S(1)}, u32[]{:S(2)}, u32[]{:S(2)}) %all-to-all-start.1) | async-done | bytes 16416 | tf_op jit(solution)/shard_map/all_to_all | solution.py:122
  64.0 28.9 %scatter_custom_fusion.2 = f32[1024]{0:T(1024)S(1)} fusion(s32[4096]{0:T(1024)} %reshape.500, f32[4096]{0:T(1024)S(1)} %reshape.502, f32[]{:T(128)} %constant.251.clone.1), kind=kCustom, calls=%fused_computation.635 | custom fusion | flops 4096 | bytes 4608
  102.4 3.5 collective-permute-start.3
  120.0 3.1 collective-permute-start.7
  123.1 5.1 %collective-permute-start.6 = (f32[2,32,1,128]{3,1,2,0:T(8,128)S(1)}, f32[2,32,1,128]{3,1,2,0:T(8,128)S(1)}, u32[]{:S(2)}, u32[]{:S(2)}) collective-permute-start(f32[2,32,1,128]{3,1,2,0:T(8,128)S(1)} %pad_maximum_fusion.63), channel_id=1, source_target_pairs={{0,1},{1,2},{2,3},{3,4},{4,5},{5,6},{6,7},{7,8},{8,9},{9,10},{10,1... | collective-permute-start | bytes 98312 | tf_op jit(solution)/shard_map/ppermute | solution.py:25
  140.7 5.8 %collective-permute-start.10 = (f32[2,32,1,128]{3,1,2,0:T(8,128)S(1)}, f32[2,32,1,128]{3,1,2,0:T(8,128)S(1)}, u32[]{:S(2)}, u32[]{:S(2)}) collective-permute-start(f32[2,32,1,128]{3,1,2,0:T(8,128)S(1)} %pad_maximum_fusion.67), channel_id=1, source_target_pairs={{0,1},{1,2},{2,3},{3,4},{4,5},{5,6},{6,7},{7,8},{8,9},{9,10},{10,1... | collective-permute-start | bytes 98312 | tf_op jit(solution)/shard_map/ppermute | solution.py:25
  156.1 5.4 %collective-permute-start.14 = (f32[2,32,1,128]{3,1,2,0:T(8,128)S(1)}, f32[2,32,1,128]{3,1,2,0:T(8,128)S(1)}, u32[]{:S(2)}, u32[]{:S(2)}) collective-permute-start(f32[2,32,1,128]{3,1,2,0:T(8,128)S(1)} %pad_maximum_fusion.71), channel_id=1, source_target_pairs={{0,1},{1,2},{2,3},{3,4},{4,5},{5,6},{6,7},{7,8},{8,9},{9,10},{10,1... | collective-permute-start | bytes 98312 | tf_op jit(solution)/shard_map/ppermute | solution.py:25
  161.5 3.1 collective-permute-start.15
  173.1 3.1 bitcast_dynamic-update-slice_fusion.3
  177.8 152.3 %all-reduce.45.cloned.1.call-done = f32[2,2,256,256]{3,2,1,0:T(8,128)} async-done(((f32[2,2,256,256]{3,2,1,0:T(8,128)}), f32[2,2,256,256]{3,2,1,0:T(8,128)}) %all-reduce.45.cloned.1.call-update) | async-done | bytes 1048592 | tf_op jit(solution)/shard_map/psum | solution.py:171
  341.5 3.0 fusion.94
  356.4 4.0 fusion.98
  360.5 4.0 collective-permute-start.23
  364.5 4.2 collective-permute-start.22
  378.1 4.0 collective-permute-start.27
  382.2 5.7 %collective-permute-start.26 = (f32[2,32,1,128]{3,1,2,0:T(8,128)S(1)}, f32[2,32,1,128]{3,1,2,0:T(8,128)S(1)}, u32[]{:S(2)}, u32[]{:S(2)}) collective-permute-start(f32[2,32,1,128]{3,1,2,0:T(8,128)S(1)} %pad_maximum_fusion.85), channel_id=1, source_target_pairs={{0,1},{1,2},{2,3},{3,4},{4,5},{5,6},{6,7},{7,8},{8,9},{9,10},{10,1... | collective-permute-start | bytes 98312 | tf_op jit(solution)/shard_map/ppermute | solution.py:25
  400.3 5.7 %collective-permute-start.30 = (f32[2,32,1,128]{3,1,2,0:T(8,128)S(1)}, f32[2,32,1,128]{3,1,2,0:T(8,128)S(1)}, u32[]{:S(2)}, u32[]{:S(2)}) collective-permute-start(f32[2,32,1,128]{3,1,2,0:T(8,128)S(1)} %pad_maximum_fusion.89), channel_id=1, source_target_pairs={{0,1},{1,2},{2,3},{3,4},{4,5},{5,6},{6,7},{7,8},{8,9},{9,10},{10,1... | collective-permute-start | bytes 98312 | tf_op jit(solution)/shard_map/ppermute | solution.py:25
  407.0 5.4 %fusion.147 = f32[32,32]{1,0:T(8,128)S(1)} fusion(f32[32,32,128]{2,1,0:T(8,128)S(1)} %copy-done.26, f32[32,32,128]{2,1,0:T(8,128)S(1)} %get-tuple-element.164, f32[1,32,128]{2,1,0:T(8,128)S(1)} %get-tuple-element.191, f32[32,32,128]{2,1,0:T(8,128)S(1)} %get-tuple-element.163, f32[32,1,128]{2,1,0:T(1,128)S(1)} %bitcast.473, ...), kind=kLoop, calls=%fused_computation.197 | loop fusion | flops 265216 | bytes 18419712 | tf_op jit(solution)/shard_map/reduce_sum | solution.py:195
  412.5 27.6 %gather_fusion = f32[4096]{0:T(1024)S(1)} fusion(f32[32,32]{0,1:T(8,128)S(1)} %copy.5037, s32[4096]{0:T(1024)S(1)} %reshape.470), kind=kCustom, calls=%fused_computation | custom fusion | bytes 65536 | tf_op jit(solution)/shard_map/gather | solution.py:196
  441.0 19.8 %all-to-all-start.2 = ((f32[128,2,16]{2,1,0:T(2,128)}), f32[128,2,16]{2,1,0:T(2,128)S(1)}, u32[]{:S(2)}, u32[]{:S(2)}) async-start(f32[128,2,16]{2,1,0:T(2,128)} %reshape.462), calls=%async_computation.2 | async-start | bytes 262144 | tf_op jit(solution)/shard_map/all_to_all | solution.py:197
  463.0 8.0 %all-to-all-done.2 = f32[128,2,16]{2,1,0:T(2,128)S(1)} async-done(((f32[128,2,16]{2,1,0:T(2,128)}), f32[128,2,16]{2,1,0:T(2,128)S(1)}, u32[]{:S(2)}, u32[]{:S(2)}) %all-to-all-start.2) | async-done | bytes 16416 | tf_op jit(solution)/shard_map/all_to_all | solution.py:197
  (386 shorter events, 127.0 us)
Async XLA Ops:
  7.2 85.9 %collective-permute-start.16 = (f32[2,1,32,128]{3,2,1,0:T(8,128)S(1)}, f32[2,1,32,128]{3,2,1,0:T(8,128)}, u32[]{:S(2)}, u32[]{:S(2)}) collective-permute-start(f32[2,1,32,128]{3,2,1,0:T(8,128)S(1)} %stack.374), channel_id=1, source_target_pairs={{16,0},{32,16},{48,32},{64,48},{80,64},{96,80},{112,96},{17,1},{33... | collective-permute-start | bytes 98312 | tf_op jit(solution)/shard_map/ppermute | solution.py:25
  9.4 84.6 %collective-permute-start.17 = (f32[2,32,1,128]{3,1,2,0:T(8,128)}, f32[2,32,1,128]{3,1,2,0:T(8,128)}, u32[]{:S(2)}, u32[]{:S(2)}) collective-permute-start(f32[2,32,1,128]{3,1,2,0:T(8,128)} %stack.375), channel_id=1, source_target_pairs={{1,0},{2,1},{3,2},{4,3},{5,4},{6,5},{7,6},{8,7},{9,8},{10,9},{11,1... | collective-permute-start | bytes 98312 | tf_op jit(solution)/shard_map/ppermute | solution.py:25
  18.3 23.9 %all-to-all-start = ((f32[128,2,2]{1,2,0:T(2,128)}), f32[128,2,2]{1,2,0:T(2,128)S(1)}, u32[]{:S(2)}, u32[]{:S(2)}) async-start(f32[128,2,2]{1,2,0:T(2,128)} %copy.4958), calls=%async_computation | async-start | bytes 262144 | tf_op jit(solution)/shard_map/all_to_all | solution.py:129
  34.6 65.6 %collective-permute-start.1 = (f32[2,32,1,128]{3,1,2,0:T(8,128)}, f32[2,32,1,128]{3,1,2,0:T(8,128)}, u32[]{:S(2)}, u32[]{:S(2)}) collective-permute-start(f32[2,32,1,128]{3,1,2,0:T(8,128)} %pad_maximum_fusion.58), channel_id=1, source_target_pairs={{1,0},{2,1},{3,2},{4,3},{5,4},{6,5},{7,6},{8,7},{9,8},{10,9},{11,1... | collective-permute-start | bytes 98312 | tf_op jit(solution)/shard_map/ppermute | solution.py:25
  38.1 62.8 %collective-permute-start = (f32[2,1,32,128]{3,2,1,0:T(8,128)}, f32[2,1,32,128]{3,2,1,0:T(8,128)}, u32[]{:S(2)}, u32[]{:S(2)}) collective-permute-start(f32[2,1,32,128]{3,2,1,0:T(8,128)} %stack.314), channel_id=1, source_target_pairs={{16,0},{32,16},{48,32},{64,48},{80,64},{96,80},{112,96},{17,1},{33... | collective-permute-start | bytes 98312 | tf_op jit(solution)/shard_map/ppermute | solution.py:25
  42.3 21.6 %all-to-all-start.1 = ((f32[128,2,16]{2,1,0:T(2,128)}), f32[128,2,16]{2,1,0:T(2,128)S(1)}, u32[]{:S(2)}, u32[]{:S(2)}) async-start(f32[128,2,16]{2,1,0:T(2,128)} %bitcast.24), calls=%async_computation.1 | async-start | bytes 262144 | tf_op jit(solution)/shard_map/all_to_all | solution.py:122
  53.7 276.5 %all-reduce.45.cloned.1.call-start = ((), (), s32[]{:S(2)}) async-start(), calls=%async_computation.3 | async-start | bytes 2097152 | tf_op jit(solution)/shard_map/psum | solution.py:171
  95.3 13.2 %collective-permute-start.18 = (f32[2,32,1,128]{3,1,2,0:T(8,128)S(1)}, f32[2,32,1,128]{3,1,2,0:T(8,128)S(1)}, u32[]{:S(2)}, u32[]{:S(2)}) collective-permute-start(f32[2,32,1,128]{3,1,2,0:T(8,128)S(1)} %pad_maximum_fusion.77), channel_id=1, source_target_pairs={{0,1},{1,2},{2,3},{3,4},{4,5},{5,6},{6,7},{7,8},{8,9},{9,10},{10,1... | collective-permute-start | bytes 98312 | tf_op jit(solution)/shard_map/ppermute | solution.py:25
  98.0 11.2 %collective-permute-start.19 = (f32[2,1,32,128]{3,2,1,0:T(8,128)S(1)}, f32[2,1,32,128]{3,2,1,0:T(8,128)S(1)}, u32[]{:S(2)}, u32[]{:S(2)}) collective-permute-start(f32[2,1,32,128]{3,2,1,0:T(8,128)S(1)} %pad_maximum_fusion.78), channel_id=1, source_target_pairs={{0,16},{16,32},{32,48},{48,64},{64,80},{80,96},{96,112},{1,17},{17... | collective-permute-start | bytes 98312 | tf_op jit(solution)/shard_map/ppermute | solution.py:25
  102.4 7.7 %collective-permute-start.3 = (f32[2,1,32,128]{3,2,1,0:T(8,128)S(1)}, f32[2,1,32,128]{3,2,1,0:T(8,128)S(1)}, u32[]{:S(2)}, u32[]{:S(2)}) collective-permute-start(f32[2,1,32,128]{3,2,1,0:T(8,128)S(1)} %pad_maximum_fusion.60), channel_id=1, source_target_pairs={{0,16},{16,32},{32,48},{48,64},{64,80},{80,96},{96,112},{1,17},{17... | collective-permute-start | bytes 98312 | tf_op jit(solution)/shard_map/ppermute | solution.py:25
  120.0 8.2 %collective-permute-start.7 = (f32[2,1,32,128]{3,2,1,0:T(8,128)S(1)}, f32[2,1,32,128]{3,2,1,0:T(8,128)S(1)}, u32[]{:S(2)}, u32[]{:S(2)}) collective-permute-start(f32[2,1,32,128]{3,2,1,0:T(8,128)S(1)} %pad_maximum_fusion.64), channel_id=1, source_target_pairs={{0,16},{16,32},{32,48},{48,64},{64,80},{80,96},{96,112},{1,17},{17... | collective-permute-start | bytes 98312 | tf_op jit(solution)/shard_map/ppermute | solution.py:25
  123.1 6.1 %collective-permute-start.6 = (f32[2,32,1,128]{3,1,2,0:T(8,128)S(1)}, f32[2,32,1,128]{3,1,2,0:T(8,128)S(1)}, u32[]{:S(2)}, u32[]{:S(2)}) collective-permute-start(f32[2,32,1,128]{3,1,2,0:T(8,128)S(1)} %pad_maximum_fusion.63), channel_id=1, source_target_pairs={{0,1},{1,2},{2,3},{3,4},{4,5},{5,6},{6,7},{7,8},{8,9},{9,10},{10,1... | collective-permute-start | bytes 98312 | tf_op jit(solution)/shard_map/ppermute | solution.py:25
  137.9 8.6 %collective-permute-start.11 = (f32[2,1,32,128]{3,2,1,0:T(8,128)S(1)}, f32[2,1,32,128]{3,2,1,0:T(8,128)S(1)}, u32[]{:S(2)}, u32[]{:S(2)}) collective-permute-start(f32[2,1,32,128]{3,2,1,0:T(8,128)S(1)} %pad_maximum_fusion.68), channel_id=1, source_target_pairs={{0,16},{16,32},{32,48},{48,64},{64,80},{80,96},{96,112},{1,17},{17... | collective-permute-start | bytes 98312 | tf_op jit(solution)/shard_map/ppermute | solution.py:25
  140.7 6.7 %collective-permute-start.10 = (f32[2,32,1,128]{3,1,2,0:T(8,128)S(1)}, f32[2,32,1,128]{3,1,2,0:T(8,128)S(1)}, u32[]{:S(2)}, u32[]{:S(2)}) collective-permute-start(f32[2,32,1,128]{3,1,2,0:T(8,128)S(1)} %pad_maximum_fusion.67), channel_id=1, source_target_pairs={{0,1},{1,2},{2,3},{3,4},{4,5},{5,6},{6,7},{7,8},{8,9},{9,10},{10,1... | collective-permute-start | bytes 98312 | tf_op jit(solution)/shard_map/ppermute | solution.py:25
  156.1 8.5 %collective-permute-start.14 = (f32[2,32,1,128]{3,1,2,0:T(8,128)S(1)}, f32[2,32,1,128]{3,1,2,0:T(8,128)S(1)}, u32[]{:S(2)}, u32[]{:S(2)}) collective-permute-start(f32[2,32,1,128]{3,1,2,0:T(8,128)S(1)} %pad_maximum_fusion.71), channel_id=1, source_target_pairs={{0,1},{1,2},{2,3},{3,4},{4,5},{5,6},{6,7},{7,8},{8,9},{9,10},{10,1... | collective-permute-start | bytes 98312 | tf_op jit(solution)/shard_map/ppermute | solution.py:25
  344.5 11.8 %collective-permute-start.21 = (f32[2,32,1,128]{3,1,2,0:T(8,128)S(1)}, f32[2,32,1,128]{3,1,2,0:T(8,128)S(1)}, u32[]{:S(2)}, u32[]{:S(2)}) collective-permute-start(f32[2,32,1,128]{3,1,2,0:T(8,128)S(1)} %pad_maximum_fusion.80), channel_id=1, source_target_pairs={{1,0},{2,1},{3,2},{4,3},{5,4},{6,5},{7,6},{8,7},{9,8},{10,9},{11,1... | collective-permute-start | bytes 98312 | tf_op jit(solution)/shard_map/ppermute | solution.py:25
  347.1 9.2 %collective-permute-start.20 = (f32[2,1,32,128]{3,2,1,0:T(8,128)}, f32[2,1,32,128]{3,2,1,0:T(8,128)S(1)}, u32[]{:S(2)}, u32[]{:S(2)}) collective-permute-start(f32[2,1,32,128]{3,2,1,0:T(8,128)} %pad_maximum_fusion.79), channel_id=1, source_target_pairs={{16,0},{32,16},{48,32},{64,48},{80,64},{96,80},{112,96},{17,1},{33... | collective-permute-start | bytes 98312 | tf_op jit(solution)/shard_map/ppermute | solution.py:25
  360.5 8.2 %collective-permute-start.23 = (f32[2,1,32,128]{3,2,1,0:T(8,128)S(1)}, f32[2,1,32,128]{3,2,1,0:T(8,128)S(1)}, u32[]{:S(2)}, u32[]{:S(2)}) collective-permute-start(f32[2,1,32,128]{3,2,1,0:T(8,128)S(1)} %pad_maximum_fusion.82), channel_id=1, source_target_pairs={{0,16},{16,32},{32,48},{48,64},{64,80},{80,96},{96,112},{1,17},{17... | collective-permute-start | bytes 98312 | tf_op jit(solution)/shard_map/ppermute | solution.py:25
  370.7 5.9 %collective-permute-start.25 = (f32[2,32,1,128]{3,1,2,0:T(8,128)S(1)}, f32[2,32,1,128]{3,1,2,0:T(8,128)S(1)}, u32[]{:S(2)}, u32[]{:S(2)}) collective-permute-start(f32[2,32,1,128]{3,1,2,0:T(8,128)S(1)} %pad_maximum_fusion.84), channel_id=1, source_target_pairs={{1,0},{2,1},{3,2},{4,3},{5,4},{6,5},{7,6},{8,7},{9,8},{10,9},{11,1... | collective-permute-start | bytes 98312 | tf_op jit(solution)/shard_map/ppermute | solution.py:25
  378.1 9.7 %collective-permute-start.27 = (f32[2,1,32,128]{3,2,1,0:T(8,128)S(1)}, f32[2,1,32,128]{3,2,1,0:T(8,128)S(1)}, u32[]{:S(2)}, u32[]{:S(2)}) collective-permute-start(f32[2,1,32,128]{3,2,1,0:T(8,128)S(1)} %pad_maximum_fusion.86), channel_id=1, source_target_pairs={{0,16},{16,32},{32,48},{48,64},{64,80},{80,96},{96,112},{1,17},{17... | collective-permute-start | bytes 98312 | tf_op jit(solution)/shard_map/ppermute | solution.py:25
  382.2 6.7 %collective-permute-start.26 = (f32[2,32,1,128]{3,1,2,0:T(8,128)S(1)}, f32[2,32,1,128]{3,1,2,0:T(8,128)S(1)}, u32[]{:S(2)}, u32[]{:S(2)}) collective-permute-start(f32[2,32,1,128]{3,1,2,0:T(8,128)S(1)} %pad_maximum_fusion.85), channel_id=1, source_target_pairs={{0,1},{1,2},{2,3},{3,4},{4,5},{5,6},{6,7},{7,8},{8,9},{9,10},{10,1... | collective-permute-start | bytes 98312 | tf_op jit(solution)/shard_map/ppermute | solution.py:25
  397.6 8.4 %collective-permute-start.31 = (f32[2,1,32,128]{3,2,1,0:T(8,128)S(1)}, f32[2,1,32,128]{3,2,1,0:T(8,128)S(1)}, u32[]{:S(2)}, u32[]{:S(2)}) collective-permute-start(f32[2,1,32,128]{3,2,1,0:T(8,128)S(1)} %pad_maximum_fusion.90), channel_id=1, source_target_pairs={{0,16},{16,32},{32,48},{48,64},{64,80},{80,96},{96,112},{1,17},{17... | collective-permute-start | bytes 98312 | tf_op jit(solution)/shard_map/ppermute | solution.py:25
  400.3 6.7 %collective-permute-start.30 = (f32[2,32,1,128]{3,1,2,0:T(8,128)S(1)}, f32[2,32,1,128]{3,1,2,0:T(8,128)S(1)}, u32[]{:S(2)}, u32[]{:S(2)}) collective-permute-start(f32[2,32,1,128]{3,1,2,0:T(8,128)S(1)} %pad_maximum_fusion.89), channel_id=1, source_target_pairs={{0,1},{1,2},{2,3},{3,4},{4,5},{5,6},{6,7},{7,8},{8,9},{9,10},{10,1... | collective-permute-start | bytes 98312 | tf_op jit(solution)/shard_map/ppermute | solution.py:25
  441.0 30.0 %all-to-all-start.2 = ((f32[128,2,16]{2,1,0:T(2,128)}), f32[128,2,16]{2,1,0:T(2,128)S(1)}, u32[]{:S(2)}, u32[]{:S(2)}) async-start(f32[128,2,16]{2,1,0:T(2,128)} %reshape.462), calls=%async_computation.2 | async-start | bytes 262144 | tf_op jit(solution)/shard_map/all_to_all | solution.py:197
  (67 other events, 864.0 us)
Sparse Core Ops, SparseCore 0:
  173.2 156.9 all-reduce.44
where the time goes:
time: 481 us; the launch traced here: 479 us
  waiting for transfers between devices  189 us (39%)
  starting transfers between devices  135 us (28%)
  local copies, waits for them, and re-layouts  63.3 us (13%)
  other arithmetic  62.6 us (13%)
  between operations  16.2 us (3%)
  matrix products  13.1 us (3%)
    psum x1, waiting for transfers between devices, shards(): far_field = lax.psum(partial_far, ('gx', 'gy'))  152 us
    ppermute x32, starting transfers between devices, passed_along(): return lax.ppermute(shard, axis, pairs)  91.1 us
    unnamed x7, other arithmetic  33.4 us
    gather x1, local copies, waits for them, and re-layouts, shards(): picked = column_grad[cells_x, cells_y]  27.6 us
    ppermute x32, waiting for transfers between devices, passed_along(): return lax.ppermute(shard, axis, pairs)  21.6 us
    all_to_all x1, starting transfers between devices, shards(): lax.all_to_all(picked.reshape(devices, capacity, 16), ('gx', 'gy'), split...  19.8 us
    dot_general x16, matrix products, contract(): jnp.einsum(pattern, first_op, second_op, precision=lax.Precision.HIGHEST)  13.1 us
    all_to_all x1, starting transfers between devices, shards(): lax.all_to_all(packed_at.reshape(devices, capacity, 2), ('gx', 'gy'), spl...  12.4 us
  transfers between devices with their start and end apart: 36, of which 19 were waited for; matrix products, arithmetic and copies ran while one was open for 14% of the time, Pallas kernels for 0%

commit v1 on v0

--- a/solution.py
+++ b/solution.py
@@ -70,26 +70,20 @@
     return jnp.einsum(pattern, first_op, second_op, precision=lax.Precision.HIGHEST)
 
 
-def project_forward(mon_re, mon_im, table_x, table_y, norm_scale):
-    x_re, x_im = table_x
-    y_re, y_im = table_y
-    part_re = contract("ux,cxy->cuy", x_re, mon_re) - contract("ux,cxy->cuy", x_im, mon_im)
-    part_im = contract("ux,cxy->cuy", x_re, mon_im) + contract("ux,cxy->cuy", x_im, mon_re)
-    far_re = contract("cuy,vy->cuv", part_re, y_re) - contract("cuy,vy->cuv", part_im, y_im)
-    far_im = contract("cuy,vy->cuv", part_re, y_im) + contract("cuy,vy->cuv", part_im, y_re)
-    return norm_scale * jnp.stack([far_re, far_im])
-
-
-def project_back(weighted, table_x, table_y, norm_scale):
-    x_re, x_im = table_x
-    y_re, y_im = table_y
-    w_re = weighted[0]
-    w_im = weighted[1]
-    half_re = contract("cuv,vy->cuy", w_re, y_re) - contract("cuv,vy->cuy", w_im, y_im)
-    half_im = contract("cuv,vy->cuy", w_re, y_im) + contract("cuv,vy->cuy", w_im, y_re)
-    back_re = contract("ux,cuy->cxy", x_re, half_re) - contract("ux,cuy->cxy", x_im, half_im)
-    back_im = contract("ux,cuy->cxy", x_re, half_im) + contract("ux,cuy->cxy", x_im, half_re)
-    return (2.0 * norm_scale * back_re, 2.0 * norm_scale * back_im)
+def route_pillars(rows, slot_ids, devices, capacity):
+    slots = devices * capacity
+    placing = (slot_ids[:, None] == jnp.arange(slots, dtype=jnp.int32)[None, :]).astype(
+        jnp.float32
+    )
+    packed = contract("ps,pk->sk", placing, rows)
+    got = lax.all_to_all(
+        packed.reshape(devices, capacity, rows.shape[1]),
+        ("gx", "gy"),
+        split_axis=0,
+        concat_axis=0,
+        tiled=True,
+    )
+    return placing, got.reshape(slots, rows.shape[1])
 
 
 def shards(fields, eps_background, target, widths, intersection, pillar_tile, anchors):
@@ -108,37 +102,18 @@
     earlier = jnp.cumsum(onehot, axis=0) - onehot
     order_in = jnp.sum(earlier * onehot, axis=1)
     slot_ids = target_tile * capacity + order_in
-    packed = (
-        jnp.zeros((devices * capacity, 16), jnp.float32)
-        .at[slot_ids]
-        .set(intersection * widths[:, None])
-    )
-    packed_at = (
-        jnp.zeros((devices * capacity, 2), jnp.float32)
-        .at[slot_ids]
-        .set(anchors.astype(jnp.float32))
-    )
-    got_vals, got_at = (
-        lax.all_to_all(
-            packed.reshape(devices, capacity, 16),
-            ("gx", "gy"),
-            split_axis=0,
-            concat_axis=0,
-            tiled=True,
-        ),
-        lax.all_to_all(
-            packed_at.reshape(devices, capacity, 2),
-            ("gx", "gy"),
-            split_axis=0,
-            concat_axis=0,
-            tiled=True,
-        ),
-    )
-    local_vals = got_vals.reshape(devices * capacity, 16)
-    local_at = got_at.reshape(devices * capacity, 2).astype(jnp.int32)
-    cells_x = local_at[:, 0:1] + (offsets // 4)[None, :]
-    cells_y = local_at[:, 1:2] + (offsets % 4)[None, :]
-    filling = jnp.zeros((TILE, TILE), jnp.float32).at[cells_x, cells_y].add(local_vals)
+    rows = jnp.concatenate(
+        [intersection * widths[:, None], anchors.astype(jnp.float32)], axis=1
+    )
+    placing, got = route_pillars(rows, slot_ids, devices, capacity)
+    local_vals = got[:, :16]
+    local_at = got[:, 16:18].astype(jnp.int32)
+    cells_x = (local_at[:, 0:1] + (offsets // 4)[None, :]).reshape(-1)
+    cells_y = (local_at[:, 1:2] + (offsets % 4)[None, :]).reshape(-1)
+    lanes = jnp.arange(TILE, dtype=jnp.int32)
+    pick_x = (cells_x[:, None] == lanes[None, :]).astype(jnp.float32)
+    pick_y = (cells_y[:, None] == lanes[None, :]).astype(jnp.float32)
+    filling = contract("sx,sy->xy", pick_x, pick_y * local_vals.reshape(-1)[:, None])
     z_index = jnp.arange(fields.shape[3], dtype=jnp.int32)
     layers = ((z_index >= ZM - ZP) & (z_index < ZM)).astype(jnp.float32)
     permittivity = eps_background + DELTA_EPS * filling[:, :, None] * layers[None, None, :]
@@ -163,16 +138,46 @@
             )
         )
     norm_scale = (TILE * span_x * TILE * span_y) ** (-0.5)
-    table_x = kernel_table(U, TILE * span_x, place_x * TILE, TILE)
-    table_y = kernel_table(V, TILE * span_y, place_y * TILE, TILE)
+    x_re, x_im = kernel_table(U, TILE * span_x, place_x * TILE, TILE)
+    y_re, y_im = kernel_table(V, TILE * span_y, place_y * TILE, TILE)
+    part = jnp.stack(
+        [
+            contract("ux,cxy->ucy", x_re, mon_re) - contract("ux,cxy->ucy", x_im, mon_im),
+            contract("ux,cxy->ucy", x_re, mon_im) + contract("ux,cxy->ucy", x_im, mon_re),
+        ]
+    )
+    part = lax.psum_scatter(part, "gx", scatter_dimension=1, tiled=True)
+    part_re, part_im = part[0], part[1]
+    far = jnp.stack(
+        [
+            contract("ucy,vy->cuv", part_re, y_re) - contract("ucy,vy->cuv", part_im, y_im),
+            contract("ucy,vy->cuv", part_re, y_im) + contract("ucy,vy->cuv", part_im, y_re),
+        ],
+        axis=2,
+    )
+    far = norm_scale * lax.psum_scatter(far, "gy", scatter_dimension=1, tiled=True)
     row_count = U // devices
-    row_start = linear * row_count
-    partial_far = project_forward(mon_re, mon_im, table_x, table_y, norm_scale)
-    far_field = lax.psum(partial_far, ("gx", "gy"))
-    mine_rows = lax.dynamic_slice_in_dim(far_field, row_start, row_count, 2)
-    focal_power = jnp.sum(mine_rows * mine_rows, axis=(0, 1))
-    weighted = jnp.stack([target * far_field[0], -(target * far_field[1])])
-    back_re, back_im = project_back(weighted, table_x, table_y, norm_scale)
+    focal_power = jnp.sum(far * far, axis=(0, 2))
+    mine_target = lax.dynamic_slice_in_dim(target, linear * row_count, row_count, 0)
+    weighted = jnp.stack(
+        [mine_target * far[:, :, 0], -(mine_target * far[:, :, 1])], axis=2
+    )
+    weighted = lax.all_gather(weighted, "gy", axis=1, tiled=True)
+    w_re, w_im = weighted[:, :, 0], weighted[:, :, 1]
+    half = jnp.stack(
+        [
+            contract("cuv,vy->cuy", w_re, y_re) - contract("cuv,vy->cuy", w_im, y_im),
+            contract("cuv,vy->cuy", w_re, y_im) + contract("cuv,vy->cuy", w_im, y_re),
+        ]
+    )
+    half = lax.all_gather(half, "gx", axis=2, tiled=True)
+    half_re, half_im = half[0], half[1]
+    back_re = 2.0 * norm_scale * (
+        contract("ux,cuy->cxy", x_re, half_re) - contract("ux,cuy->cxy", x_im, half_im)
+    )
+    back_im = 2.0 * norm_scale * (
+        contract("ux,cuy->cxy", x_re, half_im) + contract("ux,cuy->cxy", x_im, half_re)
+    )
     adjoint = tuple((blank for component in range(6)))
     inv_layer = inv_eps[:, :, ZM - ZP : ZM]
     grad_eps = jnp.zeros((TILE, TILE, ZP), jnp.float32)
@@ -193,11 +198,12 @@
         )
         grad_eps = grad_eps - product * inv_layer
     column_grad = jnp.sum(grad_eps, axis=2)
-    picked = column_grad[cells_x, cells_y]
+    spread = contract("sx,xy->sy", pick_x, column_grad)
+    picked = jnp.sum(spread * pick_y, axis=1).reshape(devices * capacity, 16)
     returned = lax.all_to_all(
         picked.reshape(devices, capacity, 16), ("gx", "gy"), split_axis=0, concat_axis=0, tiled=True
     )
-    own_vals = returned.reshape(devices * capacity, 16)[slot_ids]
+    own_vals = contract("ps,sk->pk", placing, returned.reshape(devices * capacity, 16))
     grad_widths = DELTA_EPS * jnp.sum(intersection * own_vals, axis=1)
     return (jnp.stack(fields_now), focal_power, grad_widths)
 

time: 481 us -> 498 us (1.035)
  blocking collectives: 0 us -> 46 us
  other arithmetic: 62.6 us -> 38.1 us
  waiting for transfers between devices: 189 us -> 210 us
  local copies, waits for them, and re-layouts: 63.3 us -> 45.5 us
  starting transfers between devices: 135 us -> 129 us
    unnamed x1 -> x4, waiting for transfers between devices: 0.02 us -> 179 us
    psum x1 -> x0, waiting for transfers between devices: 152 us -> none  [shards(): far_field = lax.psum(partial_far, ('gx', 'gy'))]
    all_gather x0 -> x2, blocking collectives: none -> 46 us  [the longest x1 24.8 us: shards(): half = lax.all_gather(half, 'gx', axis=2, tiled=True)]
    gather x2 -> x0, local copies, waits for them, and re-layouts: 28.2 us -> none  [the longest x1 27.6 us: shards(): picked = column_grad[cells_x, cells_y]]
    unnamed x7 -> x4, other arithmetic: 33.4 us -> 9.03 us
    all_to_all x2 -> x1, starting transfers between devices: 23.8 us -> 12.4 us  [route_pillars(): lax.all_to_all(packed.reshape(devices, capacity, rows.shape[1]), ('gx', '...]
    ppermute x32, starting transfers between devices: 91.1 us -> 99.5 us  [passed_along(): return lax.ppermute(shard, axis, pairs)]
    all_to_all x2 -> x1, waiting for transfers between devices: 7.17 us -> 0.01 us  [route_pillars(): lax.all_to_all(packed.reshape(devices, capacity, rows.shape[1]), ('gx', '...]
  transfers between devices with their start and end apart: 36 -> 36, of which waited for: 19 -> 18; matrix products, arithmetic and copies ran while one was open for 14% -> 9% of each run, Pallas kernels for 0% -> 0%
where the time goes in v1:
time: 498 us; the launch traced here: 496 us
  waiting for transfers between devices  210 us (42%)
  starting transfers between devices  129 us (26%)
  blocking collectives  46 us (9%)
  local copies, waits for them, and re-layouts  45.5 us (9%)
  other arithmetic  38.1 us (8%)
  between operations  16.7 us (3%)
  matrix products  10.6 us (2%)
    unnamed x4, waiting for transfers between devices  179 us
    ppermute x32, starting transfers between devices, passed_along(): return lax.ppermute(shard, axis, pairs)  99.5 us
    all_gather x1, blocking collectives, shards(): half = lax.all_gather(half, 'gx', axis=2, tiled=True)  24.8 us
    ppermute x32, waiting for transfers between devices, passed_along(): return lax.ppermute(shard, axis, pairs)  22.2 us
    all_gather x1, blocking collectives, shards(): weighted = lax.all_gather(weighted, 'gy', axis=1, tiled=True)  21.3 us
    all_to_all x1, starting transfers between devices, shards(): lax.all_to_all(picked.reshape(devices, capacity, 16), ('gx', 'gy'), split...  16.7 us
    all_to_all x1, starting transfers between devices, route_pillars(): lax.all_to_all(packed.reshape(devices, capacity, rows.shape[1]), ('gx', '...  12.4 us
    another operation x12, local copies, waits for them, and re-layouts  11.5 us
  transfers between devices with their start and end apart: 36, of which 18 were waited for; matrix products, arithmetic and copies ran while one was open for 9% of the time, Pallas kernels for 0%

profile of v1, /device:TPU:1, one launch (start us, length us, event | category | flops | bytes accessed | tf_op | source)
XLA Modules:
  0.0 495.5 jit_solution(3071838714524899108)
XLA Ops:
  9.8 3.3 collective-permute-start.17
  18.0 12.4 %all-to-all-start = ((f32[128,2,18]{2,1,0:T(2,128)}), f32[128,2,18]{2,1,0:T(2,128)S(1)}, u32[]{:S(2)}, u32[]{:S(2)}) async-start(f32[128,2,18]{2,1,0:T(2,128)} %bitcast.424), calls=%async_computation | async-start | bytes 262144 | tf_op jit(solution)/shard_map/all_to_all | solution.py:79
  55.3 4.3 collective-permute-start.19
  61.8 4.3 collective-permute-start.3
  80.3 3.2 collective-permute-start.7
  83.6 4.9 collective-permute-start.6
  98.2 4.0 collective-permute-start.11
  102.2 5.7 %collective-permute-start.10 = (f32[2,32,1,128]{3,1,2,0:T(8,128)S(1)}, f32[2,32,1,128]{3,1,2,0:T(8,128)S(1)}, u32[]{:S(2)}, u32[]{:S(2)}) collective-permute-start(f32[2,32,1,128]{3,1,2,0:T(8,128)S(1)} %pad_maximum_fusion.70), channel_id=1, source_target_pairs={{0,1},{1,2},{2,3},{3,4},{4,5},{5,6},{6,7},{7,8},{8,9},{9,10},{10,1... | collective-permute-start | bytes 98312 | tf_op jit(solution)/shard_map/ppermute | solution.py:25
  117.6 5.4 %collective-permute-start.14 = (f32[2,32,1,128]{3,1,2,0:T(8,128)S(1)}, f32[2,32,1,128]{3,1,2,0:T(8,128)S(1)}, u32[]{:S(2)}, u32[]{:S(2)}) collective-permute-start(f32[2,32,1,128]{3,1,2,0:T(8,128)S(1)} %pad_maximum_fusion.74), channel_id=1, source_target_pairs={{0,1},{1,2},{2,3},{3,4},{4,5},{5,6},{6,7},{7,8},{8,9},{9,10},{10,1... | collective-permute-start | bytes 98312 | tf_op jit(solution)/shard_map/ppermute | solution.py:25
  123.0 3.5 collective-permute-start.15
  136.8 3.0 bitcast_dynamic-update-slice_fusion.3
  140.7 40.8 %reduce-scatter.5.cloned.1.call-done = f32[32,128]{1,0:T(8,128)} async-done(((f32[256,128]{1,0:T(8,128)}), f32[32,128]{1,0:T(8,128)}) %reduce-scatter.5.cloned.1.call-update) | async-done | bytes 16400
  186.5 138.6 %all-reduce.46.cloned.1.call-done = f32[2,32,2,256]{3,1,0,2:T(8,128)} async-done(((f32[2,32,2,256]{3,1,0,2:T(8,128)}), f32[2,32,2,256]{3,1,0,2:T(8,128)}) %all-reduce.46.cloned.1.call-update) | async-done | bytes 131088
  326.4 21.3 %all_gather.6 = f32[2,32,2,256]{3,2,0,1:T(2,128)S(1)} all-gather(f32[2,2,2,256]{3,2,0,1:T(2,128)S(1)} %copy.4655), channel_id=1, replica_groups=mesh['gx'=8,'gy'=16] {'gy'}, dimensions={1}, use_global_device_ids=true | all-gather | bytes 139264 | tf_op jit(solution)/shard_map/all_gather | solution.py:165
  349.3 24.8 %all_gather.7 = f32[2,2,256,32]{3,2,1,0:T(8,128)S(1)} all-gather(f32[2,2,32,32]{3,2,1,0:T(8,128)S(1)} %pad_maximum_fusion.60), channel_id=1, replica_groups=mesh['gx'=8,'gy'=16] {'gx'}, dimensions={2}, use_global_device_ids=true | all-gather | bytes 147456 | tf_op jit(solution)/shard_map/all_gather | solution.py:173
  383.5 7.7 %collective-permute-start.21 = (f32[2,32,1,128]{3,1,2,0:T(8,128)}, f32[2,32,1,128]{3,1,2,0:T(8,128)}, u32[]{:S(2)}, u32[]{:S(2)}) collective-permute-start(f32[2,32,1,128]{3,1,2,0:T(8,128)} %pad_maximum_fusion.83), channel_id=1, source_target_pairs={{1,0},{2,1},{3,2},{4,3},{5,4},{6,5},{7,6},{8,7},{9,8},{10,9},{11,1... | collective-permute-start | bytes 98312 | tf_op jit(solution)/shard_map/ppermute | solution.py:25
  404.7 4.1 fusion.100
  408.9 4.0 collective-permute-start.23
  425.0 4.3 collective-permute-start.27
  429.3 5.7 %collective-permute-start.26 = (f32[2,32,1,128]{3,1,2,0:T(8,128)S(1)}, f32[2,32,1,128]{3,1,2,0:T(8,128)S(1)}, u32[]{:S(2)}, u32[]{:S(2)}) collective-permute-start(f32[2,32,1,128]{3,1,2,0:T(8,128)S(1)} %pad_maximum_fusion.88), channel_id=1, source_target_pairs={{0,1},{1,2},{2,3},{3,4},{4,5},{5,6},{6,7},{7,8},{8,9},{9,10},{10,1... | collective-permute-start | bytes 98312 | tf_op jit(solution)/shard_map/ppermute | solution.py:25
  447.4 5.7 %collective-permute-start.30 = (f32[2,32,1,128]{3,1,2,0:T(8,128)S(1)}, f32[2,32,1,128]{3,1,2,0:T(8,128)S(1)}, u32[]{:S(2)}, u32[]{:S(2)}) collective-permute-start(f32[2,32,1,128]{3,1,2,0:T(8,128)S(1)} %pad_maximum_fusion.92), channel_id=1, source_target_pairs={{0,1},{1,2},{2,3},{3,4},{4,5},{5,6},{6,7},{7,8},{8,9},{9,10},{10,1... | collective-permute-start | bytes 98312 | tf_op jit(solution)/shard_map/ppermute | solution.py:25
  454.3 5.4 %fusion.149 = f32[32,32]{1,0:T(8,128)S(1)} fusion(f32[32,32,128]{2,1,0:T(8,128)S(1)} %copy-done.26, f32[32,32,128]{2,1,0:T(8,128)S(1)} %get-tuple-element.168, f32[1,32,128]{2,1,0:T(8,128)S(1)} %get-tuple-element.199, f32[32,32,128]{2,1,0:T(8,128)S(1)} %get-tuple-element.167, f32[32,1,128]{2,1,0:T(1,128)S(1)} %bitcast.505, ...), kind=kLoop, calls=%fused_computation.194 | loop fusion | flops 265216 | bytes 18419712
  461.0 16.7 %all-to-all-start.1 = ((f32[128,2,16]{2,1,0:T(2,128)}), f32[128,2,16]{2,1,0:T(2,128)S(1)}, u32[]{:S(2)}, u32[]{:S(2)}) async-start(f32[128,2,16]{2,1,0:T(2,128)} %reshape_reshape.3), calls=%async_computation.1 | async-start | bytes 262144 | tf_op jit(solution)/shard_map/all_to_all | solution.py:203
  479.6 8.3 %all-to-all-done.1 = f32[128,2,16]{2,1,0:T(2,128)S(1)} async-done(((f32[128,2,16]{2,1,0:T(2,128)}), f32[128,2,16]{2,1,0:T(2,128)S(1)}, u32[]{:S(2)}, u32[]{:S(2)}) %all-to-all-start.1) | async-done | bytes 16416 | tf_op jit(solution)/shard_map/all_to_all | solution.py:203
  (390 shorter events, 137.6 us)
Async XLA Ops:
  7.8 42.7 %collective-permute-start.16 = (f32[2,1,32,128]{3,2,1,0:T(8,128)}, f32[2,1,32,128]{3,2,1,0:T(8,128)}, u32[]{:S(2)}, u32[]{:S(2)}) collective-permute-start(f32[2,1,32,128]{3,2,1,0:T(8,128)} %stack.400), channel_id=1, source_target_pairs={{16,0},{32,16},{48,32},{64,48},{80,64},{96,80},{112,96},{17,1},{33... | collective-permute-start | bytes 98312 | tf_op jit(solution)/shard_map/ppermute | solution.py:25
  9.8 41.4 %collective-permute-start.17 = (f32[2,32,1,128]{3,1,2,0:T(8,128)}, f32[2,32,1,128]{3,1,2,0:T(8,128)}, u32[]{:S(2)}, u32[]{:S(2)}) collective-permute-start(f32[2,32,1,128]{3,1,2,0:T(8,128)} %stack.401), channel_id=1, source_target_pairs={{1,0},{2,1},{3,2},{4,3},{5,4},{6,5},{7,6},{8,7},{9,8},{10,9},{11,1... | collective-permute-start | bytes 98312 | tf_op jit(solution)/shard_map/ppermute | solution.py:25
  18.0 24.8 %all-to-all-start = ((f32[128,2,18]{2,1,0:T(2,128)}), f32[128,2,18]{2,1,0:T(2,128)S(1)}, u32[]{:S(2)}, u32[]{:S(2)}) async-start(f32[128,2,18]{2,1,0:T(2,128)} %bitcast.424), calls=%async_computation | async-start | bytes 262144 | tf_op jit(solution)/shard_map/all_to_all | solution.py:79
  30.4 151.1 %reduce-scatter.5.cloned.1.call-start = ((), (), s32[]{:S(2)}) async-start(), calls=%async_computation.3 | async-start | bytes 147456
  34.3 25.3 %collective-permute-start.1 = (f32[2,32,1,128]{3,1,2,0:T(8,128)}, f32[2,32,1,128]{3,1,2,0:T(8,128)}, u32[]{:S(2)}, u32[]{:S(2)}) collective-permute-start(f32[2,32,1,128]{3,1,2,0:T(8,128)} %pad_maximum_fusion.61), channel_id=1, source_target_pairs={{1,0},{2,1},{3,2},{4,3},{5,4},{6,5},{7,6},{8,7},{9,8},{10,9},{11,1... | collective-permute-start | bytes 98312 | tf_op jit(solution)/shard_map/ppermute | solution.py:25
  37.9 22.4 %collective-permute-start = (f32[2,1,32,128]{3,2,1,0:T(8,128)}, f32[2,1,32,128]{3,2,1,0:T(8,128)}, u32[]{:S(2)}, u32[]{:S(2)}) collective-permute-start(f32[2,1,32,128]{3,2,1,0:T(8,128)} %stack.337), channel_id=1, source_target_pairs={{16,0},{32,16},{48,32},{64,48},{80,64},{96,80},{112,96},{17,1},{33... | collective-permute-start | bytes 98312 | tf_op jit(solution)/shard_map/ppermute | solution.py:25
  52.6 16.1 %collective-permute-start.18 = (f32[2,32,1,128]{3,1,2,0:T(8,128)S(1)}, f32[2,32,1,128]{3,1,2,0:T(8,128)S(1)}, u32[]{:S(2)}, u32[]{:S(2)}) collective-permute-start(f32[2,32,1,128]{3,1,2,0:T(8,128)S(1)} %pad_maximum_fusion.80), channel_id=1, source_target_pairs={{0,1},{1,2},{2,3},{3,4},{4,5},{5,6},{6,7},{7,8},{8,9},{9,10},{10,1... | collective-permute-start | bytes 98312 | tf_op jit(solution)/shard_map/ppermute | solution.py:25
  55.3 14.0 %collective-permute-start.19 = (f32[2,1,32,128]{3,2,1,0:T(8,128)S(1)}, f32[2,1,32,128]{3,2,1,0:T(8,128)S(1)}, u32[]{:S(2)}, u32[]{:S(2)}) collective-permute-start(f32[2,1,32,128]{3,2,1,0:T(8,128)S(1)} %pad_maximum_fusion.81), channel_id=1, source_target_pairs={{0,16},{16,32},{32,48},{48,64},{64,80},{80,96},{96,112},{1,17},{17... | collective-permute-start | bytes 98312 | tf_op jit(solution)/shard_map/ppermute | solution.py:25
  61.8 8.4 %collective-permute-start.3 = (f32[2,1,32,128]{3,2,1,0:T(8,128)S(1)}, f32[2,1,32,128]{3,2,1,0:T(8,128)S(1)}, u32[]{:S(2)}, u32[]{:S(2)}) collective-permute-start(f32[2,1,32,128]{3,2,1,0:T(8,128)S(1)} %pad_maximum_fusion.63), channel_id=1, source_target_pairs={{0,16},{16,32},{32,48},{48,64},{64,80},{80,96},{96,112},{1,17},{17... | collective-permute-start | bytes 98312 | tf_op jit(solution)/shard_map/ppermute | solution.py:25
  80.3 8.2 %collective-permute-start.7 = (f32[2,1,32,128]{3,2,1,0:T(8,128)S(1)}, f32[2,1,32,128]{3,2,1,0:T(8,128)S(1)}, u32[]{:S(2)}, u32[]{:S(2)}) collective-permute-start(f32[2,1,32,128]{3,2,1,0:T(8,128)S(1)} %pad_maximum_fusion.67), channel_id=1, source_target_pairs={{0,16},{16,32},{32,48},{48,64},{64,80},{80,96},{96,112},{1,17},{17... | collective-permute-start | bytes 98312 | tf_op jit(solution)/shard_map/ppermute | solution.py:25
  83.6 5.9 %collective-permute-start.6 = (f32[2,32,1,128]{3,1,2,0:T(8,128)S(1)}, f32[2,32,1,128]{3,1,2,0:T(8,128)S(1)}, u32[]{:S(2)}, u32[]{:S(2)}) collective-permute-start(f32[2,32,1,128]{3,1,2,0:T(8,128)S(1)} %pad_maximum_fusion.66), channel_id=1, source_target_pairs={{0,1},{1,2},{2,3},{3,4},{4,5},{5,6},{6,7},{7,8},{8,9},{9,10},{10,1... | collective-permute-start | bytes 98312 | tf_op jit(solution)/shard_map/ppermute | solution.py:25
  98.2 9.7 %collective-permute-start.11 = (f32[2,1,32,128]{3,2,1,0:T(8,128)S(1)}, f32[2,1,32,128]{3,2,1,0:T(8,128)S(1)}, u32[]{:S(2)}, u32[]{:S(2)}) collective-permute-start(f32[2,1,32,128]{3,2,1,0:T(8,128)S(1)} %pad_maximum_fusion.71), channel_id=1, source_target_pairs={{0,16},{16,32},{32,48},{48,64},{64,80},{80,96},{96,112},{1,17},{17... | collective-permute-start | bytes 98312 | tf_op jit(solution)/shard_map/ppermute | solution.py:25
  102.2 6.7 %collective-permute-start.10 = (f32[2,32,1,128]{3,1,2,0:T(8,128)S(1)}, f32[2,32,1,128]{3,1,2,0:T(8,128)S(1)}, u32[]{:S(2)}, u32[]{:S(2)}) collective-permute-start(f32[2,32,1,128]{3,1,2,0:T(8,128)S(1)} %pad_maximum_fusion.70), channel_id=1, source_target_pairs={{0,1},{1,2},{2,3},{3,4},{4,5},{5,6},{6,7},{7,8},{8,9},{9,10},{10,1... | collective-permute-start | bytes 98312 | tf_op jit(solution)/shard_map/ppermute | solution.py:25
  117.6 8.9 %collective-permute-start.14 = (f32[2,32,1,128]{3,1,2,0:T(8,128)S(1)}, f32[2,32,1,128]{3,1,2,0:T(8,128)S(1)}, u32[]{:S(2)}, u32[]{:S(2)}) collective-permute-start(f32[2,32,1,128]{3,1,2,0:T(8,128)S(1)} %pad_maximum_fusion.74), channel_id=1, source_target_pairs={{0,1},{1,2},{2,3},{3,4},{4,5},{5,6},{6,7},{7,8},{8,9},{9,10},{10,1... | collective-permute-start | bytes 98312 | tf_op jit(solution)/shard_map/ppermute | solution.py:25
  136.7 188.3 %all-reduce.46.cloned.1.call-start = ((), (), s32[]{:S(2)}) async-start(), calls=%async_computation.4 | async-start | bytes 262144
  383.5 19.6 %collective-permute-start.21 = (f32[2,32,1,128]{3,1,2,0:T(8,128)}, f32[2,32,1,128]{3,1,2,0:T(8,128)}, u32[]{:S(2)}, u32[]{:S(2)}) collective-permute-start(f32[2,32,1,128]{3,1,2,0:T(8,128)} %pad_maximum_fusion.83), channel_id=1, source_target_pairs={{1,0},{2,1},{3,2},{4,3},{5,4},{6,5},{7,6},{8,7},{9,8},{10,9},{11,1... | collective-permute-start | bytes 98312 | tf_op jit(solution)/shard_map/ppermute | solution.py:25
  392.6 11.4 %collective-permute-start.20 = (f32[2,1,32,128]{3,2,1,0:T(8,128)}, f32[2,1,32,128]{3,2,1,0:T(8,128)}, u32[]{:S(2)}, u32[]{:S(2)}) collective-permute-start(f32[2,1,32,128]{3,2,1,0:T(8,128)} %pad_maximum_fusion.82), channel_id=1, source_target_pairs={{16,0},{32,16},{48,32},{64,48},{80,64},{96,80},{112,96},{17,1},{33... | collective-permute-start | bytes 98312 | tf_op jit(solution)/shard_map/ppermute | solution.py:25
  408.9 6.5 %collective-permute-start.23 = (f32[2,1,32,128]{3,2,1,0:T(8,128)S(1)}, f32[2,1,32,128]{3,2,1,0:T(8,128)S(1)}, u32[]{:S(2)}, u32[]{:S(2)}) collective-permute-start(f32[2,1,32,128]{3,2,1,0:T(8,128)S(1)} %pad_maximum_fusion.85), channel_id=1, source_target_pairs={{0,16},{16,32},{32,48},{48,64},{64,80},{80,96},{96,112},{1,17},{17... | collective-permute-start | bytes 98312 | tf_op jit(solution)/shard_map/ppermute | solution.py:25
  417.4 5.9 %collective-permute-start.25 = (f32[2,32,1,128]{3,1,2,0:T(8,128)S(1)}, f32[2,32,1,128]{3,1,2,0:T(8,128)S(1)}, u32[]{:S(2)}, u32[]{:S(2)}) collective-permute-start(f32[2,32,1,128]{3,1,2,0:T(8,128)S(1)} %pad_maximum_fusion.87), channel_id=1, source_target_pairs={{1,0},{2,1},{3,2},{4,3},{5,4},{6,5},{7,6},{8,7},{9,8},{10,9},{11,1... | collective-permute-start | bytes 98312 | tf_op jit(solution)/shard_map/ppermute | solution.py:25
  425.0 10.0 %collective-permute-start.27 = (f32[2,1,32,128]{3,2,1,0:T(8,128)S(1)}, f32[2,1,32,128]{3,2,1,0:T(8,128)S(1)}, u32[]{:S(2)}, u32[]{:S(2)}) collective-permute-start(f32[2,1,32,128]{3,2,1,0:T(8,128)S(1)} %pad_maximum_fusion.89), channel_id=1, source_target_pairs={{0,16},{16,32},{32,48},{48,64},{64,80},{80,96},{96,112},{1,17},{17... | collective-permute-start | bytes 98312 | tf_op jit(solution)/shard_map/ppermute | solution.py:25
  429.3 6.7 %collective-permute-start.26 = (f32[2,32,1,128]{3,1,2,0:T(8,128)S(1)}, f32[2,32,1,128]{3,1,2,0:T(8,128)S(1)}, u32[]{:S(2)}, u32[]{:S(2)}) collective-permute-start(f32[2,32,1,128]{3,1,2,0:T(8,128)S(1)} %pad_maximum_fusion.88), channel_id=1, source_target_pairs={{0,1},{1,2},{2,3},{3,4},{4,5},{5,6},{6,7},{7,8},{8,9},{9,10},{10,1... | collective-permute-start | bytes 98312 | tf_op jit(solution)/shard_map/ppermute | solution.py:25
  444.7 8.4 %collective-permute-start.31 = (f32[2,1,32,128]{3,2,1,0:T(8,128)S(1)}, f32[2,1,32,128]{3,2,1,0:T(8,128)S(1)}, u32[]{:S(2)}, u32[]{:S(2)}) collective-permute-start(f32[2,1,32,128]{3,2,1,0:T(8,128)S(1)} %pad_maximum_fusion.93), channel_id=1, source_target_pairs={{0,16},{16,32},{32,48},{48,64},{64,80},{80,96},{96,112},{1,17},{17... | collective-permute-start | bytes 98312 | tf_op jit(solution)/shard_map/ppermute | solution.py:25
  447.4 6.7 %collective-permute-start.30 = (f32[2,32,1,128]{3,1,2,0:T(8,128)S(1)}, f32[2,32,1,128]{3,1,2,0:T(8,128)S(1)}, u32[]{:S(2)}, u32[]{:S(2)}) collective-permute-start(f32[2,32,1,128]{3,1,2,0:T(8,128)S(1)} %pad_maximum_fusion.92), channel_id=1, source_target_pairs={{0,1},{1,2},{2,3},{3,4},{4,5},{5,6},{6,7},{7,8},{8,9},{9,10},{10,1... | collective-permute-start | bytes 98312 | tf_op jit(solution)/shard_map/ppermute | solution.py:25
  461.0 26.9 %all-to-all-start.1 = ((f32[128,2,16]{2,1,0:T(2,128)}), f32[128,2,16]{2,1,0:T(2,128)S(1)}, u32[]{:S(2)}, u32[]{:S(2)}) async-start(f32[128,2,16]{2,1,0:T(2,128)} %reshape_reshape.3), calls=%async_computation.1 | async-start | bytes 262144 | tf_op jit(solution)/shard_map/all_to_all | solution.py:203
  (68 other events, 765.4 us)
Sparse Core Ops, SparseCore 0:
  136.9 44.6 reduce-scatter.4
  184.7 140.2 all-reduce.45
